TPU v7x, 32 devices: a whole 2x2x4 slice. The times are simulated.
32 devices in a mesh: space: 4 (over y, core), mode: 8 (over z, x).
Axes of the slice: x: 2, y: 2, z: 4, core: 2. Of those that a mesh axis runs over, the one named last changes fastest.
Arguments:
- intensity: float32 [1024, 8, 64, 256], P('mode', None, 'space'), may hold values from 0.1 to 2
- dir_cos: float32 [3, 32], replicated, may hold values from -1 to 1, as said below
- velocity: float32 [32], replicated, may hold values from 0.2 to 1
- rate: float32 [32], replicated, may hold values from 0.05 to 2
- spectrum: float32 [32], replicated, may hold values from 0.2 to 2
- weight: float32 [32], replicated, may hold values from 0.25 to 1.75
- heat: float32 [64, 256], P('space'), may hold values from 0.5 to 4
- rough_cells: int32 [4096], P('space'), may hold values from 0 to 4095, as said below
- rough_count: int32 [4], P('space'), may hold values from 256 to 1024, as said below
- rough_map: int32 [4096, 16], P('space'), may hold values from 0 to 15
Outputs:
- intensity_new: float32 [1024, 8, 64, 256], P('mode', None, 'space')
- energy_new: float32 [8, 64, 256], P(None, 'space')
Inputs may be any that keep to these rules, and one draw needn't show every extreme that they name: `dir_cos`: even directions have a positive third cosine, and direction 2k+1 equals direction 2k with the third cosine negated; every direction has a third cosine of magnitude 0.3 or more. `rough_cells`: the entries of one index of space are distinct. `rough_count`: some index of space has all 1024 slots live.
All inputs are finite; a program needn't handle non-finite values.
Results may differ from a plain program's by a relative error of at most 0.0015.
Values sent between devices are 32-bit elements; how exact they have to be, the bound alone decides.
A program may use at most 128 MiB of HBM per device.

v0:
```python
import jax
import jax.numpy as jnp
from jax import lax
from jax.sharding import PartitionSpec as P

PAIRS = 1024


def extended(block, sides, width):
    for axis, dim in sides:
        count = lax.axis_size(axis)
        forward = [(i, i + 1) for i in range(count - 1)]
        backward = [(target, source) for source, target in forward]
        low = lax.ppermute(
            lax.slice_in_dim(block, block.shape[dim] - width, None, axis=dim), axis, forward
        )
        high = lax.ppermute(lax.slice_in_dim(block, 0, width, axis=dim), axis, backward)
        block = jnp.concatenate([low, block, high], axis=dim)
    return block


def squash(energy):
    return energy / (1.0 + 0.3 * jnp.abs(energy))


def per_device(
    intensity, dir_cos, velocity, rate, spectrum, weight, heat, rough_cells, rough_count, rough_map
):
    pairs_local = intensity.shape[0]
    modes = velocity.shape[0]
    planes_count, rows, width = (intensity.shape[1], intensity.shape[2], intensity.shape[3])
    dirs_local = pairs_local // modes
    half = dirs_local // 2
    position = lax.axis_index("mode")
    cos_local = lax.dynamic_slice_in_dim(dir_cos, position * dirs_local, dirs_local, 1)
    weight_local = lax.dynamic_slice_in_dim(weight, position * dirs_local, dirs_local, 0)
    field = intensity.reshape(dirs_local, modes, planes_count, rows, width)
    partial_value = jnp.einsum("s,smzxy->zxy", weight_local, field)
    energy = lax.psum(partial_value, "mode") / PAIRS
    equil = squash(energy)
    padded = extended(field, (("space", 3),), 1)
    ox = cos_local[0][:, None, None, None, None]
    oy = cos_local[1][:, None, None, None, None]
    speed = velocity[None, :, None, None, None]
    pady = jnp.pad(field, ((0, 0), (0, 0), (0, 0), (0, 0), (1, 1)))
    along = jnp.maximum(ox, 0.0) * (field - padded[:, :, :, :-2]) + jnp.minimum(ox, 0.0) * (
        padded[:, :, :, 2:] - field
    )
    across = jnp.maximum(oy, 0.0) * (field - pady[..., :-2]) + jnp.minimum(oy, 0.0) * (
        pady[..., 2:] - field
    )
    source = (rate * spectrum)[:, None, None, None] * equil[None]
    rhs = field + source[None] - speed * (along + across)
    diag = 1.0 + rate
    couple = velocity[None, :] * jnp.abs(cos_local[2])[:, None]
    cdown = couple[1::2][:, :, None, None]
    adown = diag[None, :, None, None] + cdown
    down_rhs = rhs[1::2]
    carry = spectrum[None, :, None, None] * heat[None, None]
    planes = [None] * planes_count
    for level in reversed(range(planes_count)):
        carry = (down_rhs[:, :, level] + cdown * carry) / adown
        planes[level] = carry
    down_new = jnp.stack(planes, axis=2)
    bottom = down_new[:, :, 0].reshape(half, modes, rows * width)
    slots = rough_cells.shape[0]
    live = jnp.arange(slots, dtype=jnp.int32) < rough_count[0]
    everything = lax.all_gather(bottom, "mode", axis=0, tiled=True)
    values = everything[:, :, rough_cells]
    targets = lax.dynamic_slice_in_dim(rough_map, position * half, half, 1)
    picked = jnp.take_along_axis(values.transpose(2, 0, 1), targets[:, :, None], axis=1).transpose(
        1, 2, 0
    )
    current = bottom[:, :, rough_cells]
    inflow = 0.9 * bottom.at[:, :, rough_cells].set(jnp.where(live[None, None, :], picked, current))
    carry = inflow.reshape(half, modes, rows, width)
    cup = couple[0::2][:, :, None, None]
    aup = diag[None, :, None, None] + cup
    up_rhs = rhs[0::2]
    planes = []
    for level in range(planes_count):
        carry = (up_rhs[:, :, level] + cup * carry) / aup
        planes.append(carry)
    up_new = jnp.stack(planes, axis=2)
    fresh = jnp.stack([up_new, down_new], axis=1).reshape(
        dirs_local, modes, planes_count, rows, width
    )
    energy_new = lax.psum(jnp.einsum("s,smzxy->zxy", weight_local, fresh), "mode") / PAIRS
    return (fresh.reshape(pairs_local, planes_count, rows, width), energy_new)


def solution(mesh):
    in_specs = (
        P("mode", None, "space", None),
        P(),
        P(),
        P(),
        P(),
        P(),
        P("space", None),
        P("space"),
        P("space"),
        P("space", None),
    )
    out_specs = (P("mode", None, "space", None), P(None, "space", None))
    return jax.shard_map(
        per_device, mesh=mesh, in_specs=in_specs, out_specs=out_specs, check_vma=False
    )
```

profile of v0, /device:TPU:0, one launch (start us, length us, event | category | flops | bytes accessed | tf_op | source)
XLA Modules:
  0.0 554.9 jit_solution(16689023233069573652)
XLA Ops:
  7.2 7.9 %bitcast_reduce_fusion = bf16[4,8,16,256]{3,2,1,0:T(8,128)(2,1)S(1)} fusion(f32[128,8,16,256]{3,2,1,0:T(8,128)} %param.10), kind=kLoop, calls=%fused_computation.96 | loop fusion | flops 4063232 | bytes 17039360 | tf_op jit(solution)/shard_map/s,smzxy->zxy/reduce_sum | solution.py:38
  15.2 0.4 fusion.23
  15.5 0.7 copy.266
  16.3 8.0 %fusion.37 = (f32[4,32,8,1,256]{4,3,2,1,0:T(1,128)S(1)}, f32[4,32,8,1,256]{4,3,2,1,0:T(1,128)S(1)}) fusion(f32[4,32,8,16,256]{4,3,2,1,0:T(8,128)} %bitcast.67), kind=kLoop, calls=%fused_computation.99 | loop fusion | bytes 4194304 | tf_op jit(solution)/shard_map/slice | solution.py:15
  24.4 2.5 collective-permute-start
  26.9 1.0 copy.238
  27.9 1.5 collective-permute-start.1
  29.6 0.9 broadcast_multiply_fusion.3
  30.6 59.0 %all-reduce.4.cloned.1.call-done = f32[8,16,256]{2,1,0:T(8,128)} async-done(((f32[8,16,256]{2,1,0:T(8,128)}), f32[8,16,256]{2,1,0:T(8,128)}) %all-reduce.4.cloned.1.call-update) | async-done | bytes 131088 | tf_op jit(solution)/shard_map/psum | solution.py:39
  89.6 0.9 add_divide_fusion.8
  90.5 0.6 broadcast_multiply_fusion.1
  91.2 1.1 copy.237
  92.3 2.3 copy.239
  94.6 34.3 %fusion.5 = f32[4,32,8,16,256]{4,3,2,1,0:T(8,128)} fusion(f32[4,32,8,16,256]{4,3,2,1,0:T(8,128)} %bitcast.68, f32[4,32,8,1,256]{4,3,2,1,0:T(1,128)S(1)} %copy.239, f32[4,32,8,1,256]{4,3,2,1,0:T(1,128)S(1)} %copy.237, f32[4]{0:T(128)S(1)} %get-tuple-element.31, f32[4]{0:T(128)S(1)} %get-tuple-element.33, f32[4]{0:T(128)S(1)} %get-tuple-element.30, ...), kind=kLoop, calls=%fused_computation.11 | loop fusion | flops 67108864 | bytes 39846080 | tf_op jit(solution)/shard_map/sub | solution.py:53
  128.9 9.2 %fusion.36 = (f32[2,32,8,16,256]{4,3,2,1,0:T(8,128)}, f32[2,32,8,16,256]{4,3,2,1,0:T(8,128)S(1)}) fusion(f32[4,32,8,16,256]{4,3,2,1,0:T(8,128)} %fusion.5), kind=kLoop, calls=%fused_computation.98 | loop fusion | bytes 33554432 | tf_op jit(solution)/shard_map/slice | solution.py:79
  138.1 1.1 divide_dynamic-update-slice_fusion
  140.1 3.0 fusion.38
  143.2 3.4 copy-done.2
  146.6 2.5 squeeze.36
  149.0 2.4 squeeze.37
  151.4 2.4 squeeze.38
  153.8 2.4 squeeze.39
  156.2 2.4 squeeze.40
  158.6 1.1 squeeze.41
  160.2 4.9 add_divide_fusion.7
  165.3 0.8 bitcast_or_fusion
  166.6 0.8 and_bitcast_fusion
  168.4 5.9 %copy.244 = f32[2,32,4096]{1,0,2:T(2,128)} copy(f32[2,32,4096]{2,1,0:T(8,128)} %add_divide_fusion.7) | data formatting | bytes 2097152 | tf_op jit(solution)/shard_map/div | solution.py:62
  174.3 5.7 %gather_fusion.1 = f32[1024,2,32]{2,1,0:T(2,128)S(1)} fusion(f32[2,32,4096]{1,0,2:T(2,128)} %copy.244, s32[1024]{0:T(1024)S(1)} %get-tuple-element.27), kind=kCustom, calls=%fused_computation.1 | custom fusion | bytes 528384 | tf_op jit(solution)/shard_map/gather | solution.py:74
  180.0 108.7 %all-gather.2.cloned.1.call-done = f32[16,32,4096]{2,1,0:T(8,128)} async-done(((f32[2,32,4096]{2,1,0:T(8,128)}), f32[16,32,4096]{2,1,0:T(8,128)}) %all-gather.2.cloned.1.call-update) | async-done | bytes 8388624 | tf_op jit(solution)/shard_map/all_gather | solution.py:68
  288.8 23.2 %copy.241 = f32[16,32,4096]{1,0,2:T(8,128)} copy(f32[16,32,4096]{2,1,0:T(8,128)} %all-gather.2.cloned.1.call-done) | data formatting | bytes 16777216 | tf_op jit(solution)/shard_map/all_gather | solution.py:68
  312.0 19.9 %gather_fusion = f32[1024,16,32]{2,1,0:T(8,128)} fusion(f32[16,32,4096]{1,0,2:T(8,128)} %copy.241, s32[1024]{0:T(1024)S(1)} %get-tuple-element.27), kind=kCustom, calls=%fused_computation | custom fusion | bytes 4198400 | tf_op jit(solution)/shard_map/gather | solution.py:69
  331.9 20.6 %gather_fusion.2 = f32[2048,32]{1,0:T(8,128)S(1)} fusion(f32[1024,16,32]{2,1,0:T(8,128)} %gather_fusion, s32[2048]{0:T(1024)S(1)} %reshape.137), kind=kCustom, calls=%fused_computation.2 | custom fusion | bytes 540672 | tf_op jit(solution)/shard_map/jit(take_along_axis)/gather | solution.py:71
  352.5 3.9 fusion.22
  356.4 93.8 %scatter_fusion = f32[2,32,4096]{1,0,2:T(2,128)} fusion(f32[2,32,4096]{1,0,2:T(2,128)} %copy.244, s32[1024]{0:T(1024)S(1)} %get-tuple-element.28, f32[1024,2,32]{2,1,0:T(2,128)S(1)} %fusion.22), kind=kCustom, calls=%fused_computation.3 | custom fusion | bytes 790528 | tf_op jit(solution)/shard_map/scatter | solution.py:75
  450.2 5.8 %broadcast_multiply_fusion = f32[2,32,4096]{1,0,2:T(2,128)} fusion(f32[2,32,4096]{1,0,2:T(2,128)} %scatter_fusion), kind=kLoop, calls=%fused_computation.22 | loop fusion | flops 262144 | bytes 2097152 | tf_op jit(solution)/shard_map/mul | solution.py:75
  456.0 3.6 copy.254
  459.6 1.6 constant_dynamic-update-slice_fusion.6
  461.3 1.9 constant_dynamic-update-slice_fusion.5
  463.2 1.6 constant_dynamic-update-slice_fusion.4
  464.8 1.9 constant_dynamic-update-slice_fusion.3
  467.8 1.1 slice-done.2
  468.9 1.3 slice-done.3
  470.2 6.9 %fusion.32 = (bf16[2,2,8,16,256]{4,3,2,1,0:T(8,128)(2,1)S(1)}, f32[2,2,32,8,16,256]{5,4,3,2,1,0:T(8,128)}) fusion(f32[2,1,32,8,16,256]{5,4,3,2,1,0:T(8,128)S(1)} %bitcast.76, f32[2,1,32,8,16,256]{5,4,3,2,1,0:T(8,128)S(1)} %bitcast.73), kind=kLoop, calls=%fused_computation.97 | loop fusion | flops 8257536 | bytes 33816576 | tf_op jit(solution)/shard_map/s,smzxy->zxy/reduce_sum | solution.py:88
  477.1 0.4 fusion.25
  477.5 0.7 copy.265
  478.1 68.6 %all-reduce.6.cloned.1.call-done = f32[8,16,256]{2,1,0:T(8,128)} async-done(((f32[8,16,256]{2,1,0:T(8,128)}), f32[8,16,256]{2,1,0:T(8,128)}) %all-reduce.6.cloned.1.call-update) | async-done | bytes 131088 | tf_op jit(solution)/shard_map/psum | solution.py:88
  546.8 1.6 broadcast_multiply_fusion.4
  (62 shorter events, 4.0 us)
Async XLA Ops:
  7.2 22.2 %copy-start = (f32[3,32]{1,0:T(4,128)S(1)}, f32[3,32]{1,0:T(4,128)}, u32[]{:S(2)}) copy-start(f32[3,32]{1,0:T(4,128)} %param.11) | copy-start | bytes 1156
  7.2 82.4 %all-reduce.4.cloned.1.call-start = ((), (), s32[]{:S(2)}) async-start(), calls=%async_computation | async-start | bytes 262144 | tf_op jit(solution)/shard_map/psum | solution.py:39
  7.2 7.9 %copy-start.9 = (f32[32]{0:T(128)S(1)}, f32[32]{0:T(128)}, u32[]{:S(2)}) copy-start(f32[32]{0:T(128)} %param.15) | copy-start | bytes 388
  15.1 14.4 %copy-start.4 = (f32[16,256]{1,0:T(8,128)S(1)}, f32[16,256]{1,0:T(8,128)}, u32[]{:S(2)}) copy-start(f32[16,256]{1,0:T(8,128)} %param.16) | copy-start | bytes 49156
  15.1 14.4 %copy-start.7 = (f32[32]{0:T(128)S(1)}, f32[32]{0:T(128)}, u32[]{:S(2)}) copy-start(f32[32]{0:T(128)} %param.12) | copy-start | bytes 388
  15.1 14.4 %copy-start.5 = (f32[32]{0:T(128)S(1)}, f32[32]{0:T(128)}, u32[]{:S(2)}) copy-start(f32[32]{0:T(128)} %param.14) | copy-start | bytes 388
  15.1 15.3 %copy-start.8 = (f32[32]{0:T(128)S(1)}, f32[32]{0:T(128)}, u32[]{:S(2)}) copy-start(f32[32]{0:T(128)} %param.13) | copy-start | bytes 388
  16.2 272.6 %all-gather.2.cloned.1.call-start = ((), (), s32[]{:S(2)}) async-start(), calls=%async_computation.1 | async-start | bytes 9437184 | tf_op jit(solution)/shard_map/all_gather | solution.py:68
  24.4 66.8 %collective-permute-start = (f32[4,32,8,1,256]{4,2,3,1,0:T(8,128)S(1)}, f32[4,32,8,1,256]{4,2,3,1,0:T(8,128)S(1)}, u32[]{:S(2)}, u32[]{:S(2)}) collective-permute-start(f32[4,32,8,1,256]{4,2,3,1,0:T(8,128)S(1)} %copy.236), channel_id=1, source_target_pairs={{0,8},{8,16},{16,24},{1,9},{9,17},{17,25},{2,10},{10,18},{18,26},{... | collective-permute-start | bytes 3145736 | tf_op jit(solution)/shard_map/ppermute | solution.py:14
  27.9 64.4 %collective-permute-start.1 = (f32[4,32,8,1,256]{4,2,3,1,0:T(8,128)}, f32[4,32,8,1,256]{4,2,3,1,0:T(8,128)}, u32[]{:S(2)}, u32[]{:S(2)}) collective-permute-start(f32[4,32,8,1,256]{4,2,3,1,0:T(8,128)} %copy.238), channel_id=1, source_target_pairs={{8,0},{16,8},{24,16},{9,1},{17,9},{25,17},{10,2},{18,10},{26,18},{... | collective-permute-start | bytes 3145736 | tf_op jit(solution)/shard_map/ppermute | solution.py:17
  143.2 3.4 copy-start.2
  146.5 12.1 %copy-start.3 = (f32[2,32,1,16,256]{4,3,2,1,0:T(8,128)S(1)}, f32[2,32,1,16,256]{4,3,2,1,0:T(8,128)}, u32[]{:S(2)}) copy-start(f32[2,32,1,16,256]{4,3,2,1,0:T(8,128)} %get-tuple-element.21) | copy-start | bytes 3145732
  159.8 8.6 %copy-start.6 = (s32[1024]{0:T(1024)S(1)}, s32[1024]{0:T(1024)}, u32[]{:S(2)}) copy-start(s32[1024]{0:T(1024)} %param.17) | copy-start | bytes 12292
  165.0 381.7 %all-reduce.6.cloned.1.call-start = ((), (), s32[]{:S(2)}) async-start(), calls=%async_computation.2 | async-start | bytes 262144 | tf_op jit(solution)/shard_map/psum | solution.py:88
  459.6 7.1 %slice-start = ((s8[8388608]{0:T(1024)(128)(4,1)}), s8[4194304]{0:T(1024)(128)(4,1)S(1)}, s32[]{:S(2)}) async-start(s8[8388608]{0:T(1024)(128)(4,1)} %bitcast.69), calls=%async_computation.3 | async-start | bytes 8388608
  463.1 3.6 slice-start.1
  466.7 2.2 slice-start.2
  467.0 3.3 slice-start.3
  470.2 78.1 %copy-start.1 = (f32[3,32]{1,0:T(4,128)S(1)}, f32[3,32]{1,0:T(4,128)}, u32[]{:S(2)}) copy-start(f32[3,32]{1,0:T(4,128)} %param.11) | copy-start | bytes 1156
Sparse Core Ops, SparseCore 0:
  16.3 73.2 all-reduce.3
  165.2 123.5 all-gather.1
  478.3 68.4 all-reduce.5
where the time goes:
time: 558 us; the launch traced here: 555 us
  waiting for transfers between devices  236 us (42%)
  local copies, waits for them, and re-layouts  216 us (39%)
  other arithmetic  82.2 us (15%)
  between operations  14.8 us (3%)
    all_gather x1, waiting for transfers between devices, per_device(): everything = lax.all_gather(bottom, 'mode', axis=0, tiled=True)  109 us
    scatter x1, local copies, waits for them, and re-layouts, per_device(): bottom.at[:, :, rough_cells]  93.8 us
    psum x1, waiting for transfers between devices, per_device(): lax.psum(jnp.einsum('s,smzxy->zxy', weight_local, fresh), 'mode') / PAIRS  68.6 us
    psum x1, waiting for transfers between devices, per_device(): energy = lax.psum(partial_value, 'mode') / PAIRS  59 us
    sub x1, other arithmetic, per_device(): rhs = field + source[None] - speed * (along + across)  34.3 us
    all_gather x1, local copies, waits for them, and re-layouts, per_device(): everything = lax.all_gather(bottom, 'mode', axis=0, tiled=True)  23.2 us
    gather x3, local copies, waits for them, and re-layouts, per_device(): jnp.take_along_axis(values.transpose(2, 0, 1), targets[:, :, None], axis=1)  21.1 us
    gather x1, local copies, waits for them, and re-layouts, per_device(): values = everything[:, :, rough_cells]  19.9 us
  transfers between devices with their start and end apart: 5, of which 3 were waited for; matrix products, arithmetic and copies ran while one was open for 5% of the time, Pallas kernels for 0%

commit v1 on v0

--- a/solution.py
+++ b/solution.py
@@ -65,7 +65,16 @@
     bottom = down_new[:, :, 0].reshape(half, modes, rows * width)
     slots = rough_cells.shape[0]
     live = jnp.arange(slots, dtype=jnp.int32) < rough_count[0]
-    everything = lax.all_gather(bottom, "mode", axis=0, tiled=True)
+    reply, item_now = (lax.axis_size("mode"), lax.axis_index("mode"))
+    everything, left_arr = (bottom, 1)
+    while left_arr < reply:
+        m_next = lax.ppermute(
+            everything, axis_name="mode", perm=[(d, d ^ left_arr) for d in range(reply)]
+        )
+        b_now = jnp.concatenate([everything, m_next], axis=0)
+        later = jnp.concatenate([m_next, everything], axis=0)
+        everything = jnp.where(item_now & left_arr == 0, b_now, later)
+        left_arr = 2 * left_arr
     values = everything[:, :, rough_cells]
     targets = lax.dynamic_slice_in_dim(rough_map, position * half, half, 1)
     picked = jnp.take_along_axis(values.transpose(2, 0, 1), targets[:, :, None], axis=1).transpose(

time: 558 us -> 749 us (1.34)
  waiting for transfers between devices: 236 us -> 361 us
  other arithmetic: 82.2 us -> 123 us
  local copies, waits for them, and re-layouts: 216 us -> 239 us
    ppermute x0 -> x3, waiting for transfers between devices: none -> 232 us  [per_device(): lax.ppermute(everything, axis_name='mode', perm=[(d, d ^ left_arr) for d...]
    all_gather x1 -> x0, waiting for transfers between devices: 109 us -> none  [per_device(): everything = lax.all_gather(bottom, 'mode', axis=0, tiled=True)]
    concatenate x0 -> x2, local copies, waits for them, and re-layouts: none -> 46.5 us  [the longest x1 23.2 us: per_device(): b_now = jnp.concatenate([everything, m_next], axis=0)]
    select_n x0 -> x3, other arithmetic: none -> 29.9 us  [per_device(): everything = jnp.where(item_now & left_arr == 0, b_now, later)]
    all_gather x1 -> x0, local copies, waits for them, and re-layouts: 23.2 us -> none  [per_device(): everything = lax.all_gather(bottom, 'mode', axis=0, tiled=True)]
    concatenate x0 -> x1, other arithmetic: none -> 11 us  [per_device(): later = jnp.concatenate([m_next, everything], axis=0)]
  transfers between devices with their start and end apart: 5 -> 7, of which waited for: 3 -> 5; matrix products, arithmetic and copies ran while one was open for 5% -> 3% of each run, Pallas kernels for 0% -> 0%
where the time goes in v1:
time: 749 us; the launch traced here: 745 us
  waiting for transfers between devices  361 us (48%)
  local copies, waits for them, and re-layouts  239 us (32%)
  other arithmetic  123 us (16%)
  between operations  15.2 us (2%)
    ppermute x3, waiting for transfers between devices, per_device(): lax.ppermute(everything, axis_name='mode', perm=[(d, d ^ left_arr) for d...  232 us
    scatter x1, local copies, waits for them, and re-layouts, per_device(): bottom.at[:, :, rough_cells]  93.9 us
    psum x1, waiting for transfers between devices, per_device(): lax.psum(jnp.einsum('s,smzxy->zxy', weight_local, fresh), 'mode') / PAIRS  70 us
    psum x1, waiting for transfers between devices, per_device(): energy = lax.psum(partial_value, 'mode') / PAIRS  59.1 us
    sub x1, other arithmetic, per_device(): rhs = field + source[None] - speed * (along + across)  34.5 us
    select_n x3, other arithmetic, per_device(): everything = jnp.where(item_now & left_arr == 0, b_now, later)  29.9 us
    concatenate x1, local copies, waits for them, and re-layouts, per_device(): b_now = jnp.concatenate([everything, m_next], axis=0)  23.2 us
    concatenate x1, local copies, waits for them, and re-layouts, per_device(): later = jnp.concatenate([m_next, everything], axis=0)  23.2 us
  transfers between devices with their start and end apart: 7, of which 5 were waited for; matrix products, arithmetic and copies ran while one was open for 3% of the time, Pallas kernels for 0%

profile of v1, /device:TPU:0, one launch (start us, length us, event | category | flops | bytes accessed | tf_op | source)
XLA Modules:
  0.0 745.2 jit_solution(16352593027967324376)
XLA Ops:
  7.2 7.9 %bitcast_reduce_fusion = bf16[4,8,16,256]{3,2,1,0:T(8,128)(2,1)S(1)} fusion(f32[128,8,16,256]{3,2,1,0:T(8,128)} %param.10), kind=kLoop, calls=%fused_computation.101 | loop fusion | flops 4063232 | bytes 17039360 | tf_op jit(solution)/shard_map/s,smzxy->zxy/reduce_sum | solution.py:38
  16.3 8.0 %fusion.37 = (f32[4,32,8,1,256]{4,3,2,1,0:T(1,128)S(1)}, f32[4,32,8,1,256]{4,3,2,1,0:T(1,128)S(1)}) fusion(f32[4,32,8,16,256]{4,3,2,1,0:T(8,128)} %bitcast.67), kind=kLoop, calls=%fused_computation.104 | loop fusion | bytes 4194304 | tf_op jit(solution)/shard_map/slice | solution.py:15
  24.4 2.5 collective-permute-start
  26.9 1.0 copy.254
  27.9 1.3 collective-permute-start.1
  30.5 59.1 %all-reduce.4.cloned.1.call-done = f32[8,16,256]{2,1,0:T(8,128)} async-done(((f32[8,16,256]{2,1,0:T(8,128)}), f32[8,16,256]{2,1,0:T(8,128)}) %all-reduce.4.cloned.1.call-update) | async-done | bytes 131088 | tf_op jit(solution)/shard_map/psum | solution.py:39
  91.2 1.1 copy.253
  92.3 2.3 copy.255
  94.6 34.5 %fusion.5 = f32[4,32,8,16,256]{4,3,2,1,0:T(8,128)} fusion(f32[4,32,8,16,256]{4,3,2,1,0:T(8,128)} %bitcast.68, f32[4,32,8,1,256]{4,3,2,1,0:T(1,128)S(1)} %copy.255, f32[4,32,8,1,256]{4,3,2,1,0:T(1,128)S(1)} %copy.253, f32[4]{0:T(128)S(1)} %get-tuple-element.33, f32[4]{0:T(128)S(1)} %get-tuple-element.35, f32[4]{0:T(128)S(1)} %get-tuple-element.32, ...), kind=kLoop, calls=%fused_computation.11 | loop fusion | flops 67108864 | bytes 39846080 | tf_op jit(solution)/shard_map/sub | solution.py:53
  129.0 9.2 %fusion.36 = (f32[2,32,8,16,256]{4,3,2,1,0:T(8,128)}, f32[2,32,8,16,256]{4,3,2,1,0:T(8,128)S(1)}) fusion(f32[4,32,8,16,256]{4,3,2,1,0:T(8,128)} %fusion.5), kind=kLoop, calls=%fused_computation.103 | loop fusion | bytes 33554432 | tf_op jit(solution)/shard_map/slice | solution.py:88
  138.3 1.1 divide_dynamic-update-slice_fusion
  140.3 3.0 fusion.38
  143.3 3.4 copy-done.2
  146.7 2.5 squeeze.36
  149.2 2.4 squeeze.37
  151.6 2.4 squeeze.38
  154.0 2.4 squeeze.39
  156.4 2.4 squeeze.40
  158.7 1.2 squeeze.41
  159.9 1.2 squeeze.42
  161.3 4.1 add_divide_fusion.7
  166.1 22.5 %collective-permute-done.2 = f32[2,32,4096]{2,1,0:T(8,128)} collective-permute-done((f32[2,32,4096]{2,1,0:T(8,128)S(1)}, f32[2,32,4096]{2,1,0:T(8,128)}, u32[]{:S(2)}, u32[]{:S(2)}) %collective-permute-start.2) | collective-permute-done | bytes 1048608 | tf_op jit(solution)/shard_map/ppermute | solution.py:71
  188.6 1.8 maximum_select_fusion.1
  191.2 44.1 %collective-permute-done.3 = f32[4,32,4096]{2,1,0:T(8,128)} collective-permute-done((f32[4,32,4096]{2,1,0:T(8,128)S(1)}, f32[4,32,4096]{2,1,0:T(8,128)}, u32[]{:S(2)}, u32[]{:S(2)}) %collective-permute-start.3) | collective-permute-done | bytes 2097184 | tf_op jit(solution)/shard_map/ppermute | solution.py:71
  235.3 4.8 maximum_select_fusion
  240.1 1.3 collective-permute-start.4
  244.5 4.4 copy.261
  248.9 5.7 gather_fusion.1
  254.6 165.0 %collective-permute-done.4 = f32[8,32,4096]{2,1,0:T(8,128)} collective-permute-done((f32[8,32,4096]{2,1,0:T(8,128)}, f32[8,32,4096]{2,1,0:T(8,128)}, u32[]{:S(2)}, u32[]{:S(2)}) %collective-permute-start.4) | collective-permute-done | bytes 4194336 | tf_op jit(solution)/shard_map/ppermute | solution.py:71
  419.6 11.0 %pad_maximum_fusion.4 = (f32[16,32,4096]{2,1,0:T(8,128)}, f32[16,32,4096]{2,1,0:T(8,128)}) fusion(f32[8,32,4096]{2,1,0:T(8,128)} %maximum_select_fusion, f32[8,32,4096]{2,1,0:T(8,128)} %collective-permute-done.4), kind=kLoop, calls=%fused_computation.24 | loop fusion | flops 4194304 | bytes 25165824 | tf_op jit(solution)/shard_map/concatenate | solution.py:75
  430.7 23.2 %copy.257 = f32[16,32,4096]{1,0,2:T(8,128)} copy(f32[16,32,4096]{2,1,0:T(8,128)} %get-tuple-element.19) | data formatting | bytes 16777216 | tf_op jit(solution)/shard_map/concatenate | solution.py:74
  453.9 23.2 %copy.258 = f32[16,32,4096]{1,0,2:T(8,128)} copy(f32[16,32,4096]{2,1,0:T(8,128)} %get-tuple-element.18) | data formatting | bytes 16777216 | tf_op jit(solution)/shard_map/concatenate | solution.py:75
  477.1 23.3 %broadcast_select_fusion = f32[16,32,4096]{1,0,2:T(8,128)} fusion(f32[16,32,4096]{1,0,2:T(8,128)} %copy.257, f32[16,32,4096]{1,0,2:T(8,128)} %copy.258, pred[]{:T(512)S(6)} %eq.9), kind=kLoop, calls=%fused_computation.22 | loop fusion | flops 2097152 | bytes 25165824 | tf_op jit(solution)/shard_map/jit(_where)/select_n | solution.py:76
  500.4 20.1 %gather_fusion = f32[1024,16,32]{2,1,0:T(8,128)} fusion(f32[16,32,4096]{1,0,2:T(8,128)} %broadcast_select_fusion, s32[1024]{0:T(1024)S(1)} %get-tuple-element.29), kind=kCustom, calls=%fused_computation | custom fusion | bytes 4198400 | tf_op jit(solution)/shard_map/gather | solution.py:78
  520.5 20.5 %gather_fusion.2 = f32[2048,32]{1,0:T(8,128)S(1)} fusion(f32[1024,16,32]{2,1,0:T(8,128)} %gather_fusion, s32[2048]{0:T(1024)S(1)} %reshape.137), kind=kCustom, calls=%fused_computation.2 | custom fusion | bytes 540672 | tf_op jit(solution)/shard_map/jit(take_along_axis)/gather | solution.py:80
  541.0 3.9 fusion.22
  544.9 93.9 %scatter_fusion = f32[2,32,4096]{1,0,2:T(2,128)} fusion(f32[2,32,4096]{1,0,2:T(2,128)} %copy.261, s32[1024]{0:T(1024)S(1)} %get-tuple-element.30, f32[1024,2,32]{2,1,0:T(2,128)S(1)} %fusion.22), kind=kCustom, calls=%fused_computation.3 | custom fusion | bytes 790528 | tf_op jit(solution)/shard_map/scatter | solution.py:84
  638.8 5.8 broadcast_multiply_fusion
  644.6 3.6 copy.271
  648.2 1.6 constant_dynamic-update-slice_fusion.6
  649.9 1.9 constant_dynamic-update-slice_fusion.5
  651.8 1.6 constant_dynamic-update-slice_fusion.4
  653.4 1.9 constant_dynamic-update-slice_fusion.3
  656.4 1.1 slice-done.2
  657.5 1.3 slice-done.3
  658.9 6.9 fusion.32
  666.8 70.0 %all-reduce.6.cloned.1.call-done = f32[8,16,256]{2,1,0:T(8,128)} async-done(((f32[8,16,256]{2,1,0:T(8,128)}), f32[8,16,256]{2,1,0:T(8,128)}) %all-reduce.6.cloned.1.call-update) | async-done | bytes 131088 | tf_op jit(solution)/shard_map/psum | solution.py:97
  736.8 1.6 broadcast_multiply_fusion.4
  (70 shorter events, 11.0 us)
Async XLA Ops:
  7.2 22.0 %copy-start = (f32[3,32]{1,0:T(4,128)S(1)}, f32[3,32]{1,0:T(4,128)}, u32[]{:S(2)}) copy-start(f32[3,32]{1,0:T(4,128)} %param.11) | copy-start | bytes 1156
  7.2 82.4 %all-reduce.4.cloned.1.call-start = ((), (), s32[]{:S(2)}) async-start(), calls=%async_computation | async-start | bytes 262144 | tf_op jit(solution)/shard_map/psum | solution.py:39
  7.2 7.9 %copy-start.9 = (f32[32]{0:T(128)S(1)}, f32[32]{0:T(128)}, u32[]{:S(2)}) copy-start(f32[32]{0:T(128)} %param.15) | copy-start | bytes 388
  15.1 14.2 %copy-start.4 = (f32[16,256]{1,0:T(8,128)S(1)}, f32[16,256]{1,0:T(8,128)}, u32[]{:S(2)}) copy-start(f32[16,256]{1,0:T(8,128)} %param.16) | copy-start | bytes 49156
  15.1 14.2 %copy-start.7 = (f32[32]{0:T(128)S(1)}, f32[32]{0:T(128)}, u32[]{:S(2)}) copy-start(f32[32]{0:T(128)} %param.12) | copy-start | bytes 388
  15.1 14.2 %copy-start.5 = (f32[32]{0:T(128)S(1)}, f32[32]{0:T(128)}, u32[]{:S(2)}) copy-start(f32[32]{0:T(128)} %param.14) | copy-start | bytes 388
  15.1 15.2 %copy-start.8 = (f32[32]{0:T(128)S(1)}, f32[32]{0:T(128)}, u32[]{:S(2)}) copy-start(f32[32]{0:T(128)} %param.13) | copy-start | bytes 388
  16.2 720.6 %all-reduce.6.cloned.1.call-start = ((), (), s32[]{:S(2)}) async-start(), calls=%async_computation.1 | async-start | bytes 262144 | tf_op jit(solution)/shard_map/psum | solution.py:97
  24.4 66.8 %collective-permute-start = (f32[4,32,8,1,256]{4,2,3,1,0:T(8,128)S(1)}, f32[4,32,8,1,256]{4,2,3,1,0:T(8,128)S(1)}, u32[]{:S(2)}, u32[]{:S(2)}) collective-permute-start(f32[4,32,8,1,256]{4,2,3,1,0:T(8,128)S(1)} %copy.252), channel_id=1, source_target_pairs={{0,8},{8,16},{16,24},{1,9},{9,17},{17,25},{2,10},{10,18},{18,26},{... | collective-permute-start | bytes 3145736 | tf_op jit(solution)/shard_map/ppermute | solution.py:14
  27.9 64.4 %collective-permute-start.1 = (f32[4,32,8,1,256]{4,2,3,1,0:T(8,128)}, f32[4,32,8,1,256]{4,2,3,1,0:T(8,128)}, u32[]{:S(2)}, u32[]{:S(2)}) collective-permute-start(f32[4,32,8,1,256]{4,2,3,1,0:T(8,128)} %copy.254), channel_id=1, source_target_pairs={{8,0},{16,8},{24,16},{9,1},{17,9},{25,17},{10,2},{18,10},{26,18},{... | collective-permute-start | bytes 3145736 | tf_op jit(solution)/shard_map/ppermute | solution.py:17
  143.3 3.4 copy-start.2
  146.7 12.1 %copy-start.3 = (f32[2,32,1,16,256]{4,3,2,1,0:T(8,128)S(1)}, f32[2,32,1,16,256]{4,3,2,1,0:T(8,128)}, u32[]{:S(2)}) copy-start(f32[2,32,1,16,256]{4,3,2,1,0:T(8,128)} %get-tuple-element.23) | copy-start | bytes 3145732
  165.4 79.0 %copy-start.6 = (s32[1024]{0:T(1024)S(1)}, s32[1024]{0:T(1024)}, u32[]{:S(2)}) copy-start(s32[1024]{0:T(1024)} %param.17) | copy-start | bytes 12292
  165.4 23.2 %collective-permute-start.2 = (f32[2,32,4096]{2,1,0:T(8,128)S(1)}, f32[2,32,4096]{2,1,0:T(8,128)}, u32[]{:S(2)}, u32[]{:S(2)}) collective-permute-start(f32[2,32,4096]{2,1,0:T(8,128)S(1)} %add_divide_fusion.7), channel_id=1, source_target_pairs={{0,1},{1,0},{2,3},{3,2},{4,5},{5,4},{6,7},{7,6},{8,9},{9,8},{10,11... | collective-permute-start | bytes 3145736 | tf_op jit(solution)/shard_map/ppermute | solution.py:71
  190.5 44.8 %collective-permute-start.3 = (f32[4,32,4096]{2,1,0:T(8,128)S(1)}, f32[4,32,4096]{2,1,0:T(8,128)}, u32[]{:S(2)}, u32[]{:S(2)}) collective-permute-start(f32[4,32,4096]{2,1,0:T(8,128)S(1)} %maximum_select_fusion.1), channel_id=1, source_target_pairs={{0,2},{1,3},{2,0},{3,1},{4,6},{5,7},{6,4},{7,5},{8,10},{9,11},{10,... | collective-permute-start | bytes 6291464 | tf_op jit(solution)/shard_map/ppermute | solution.py:71
  240.1 179.5 %collective-permute-start.4 = (f32[8,32,4096]{2,1,0:T(8,128)}, f32[8,32,4096]{2,1,0:T(8,128)}, u32[]{:S(2)}, u32[]{:S(2)}) collective-permute-start(f32[8,32,4096]{2,1,0:T(8,128)} %maximum_select_fusion), channel_id=1, source_target_pairs={{0,4},{1,5},{2,6},{3,7},{4,0},{5,1},{6,2},{7,3},{8,12},{9,13},{10,... | collective-permute-start | bytes 12582920 | tf_op jit(solution)/shard_map/ppermute | solution.py:71
  648.2 7.1 slice-start
  651.8 3.6 slice-start.1
  655.3 2.2 slice-start.2
  655.6 3.3 slice-start.3
  658.9 79.5 %copy-start.1 = (f32[3,32]{1,0:T(4,128)S(1)}, f32[3,32]{1,0:T(4,128)}, u32[]{:S(2)}) copy-start(f32[3,32]{1,0:T(4,128)} %param.11) | copy-start | bytes 1156
Sparse Core Ops, SparseCore 0:
  16.3 73.2 all-reduce.3
  666.9 69.8 all-reduce.5
